TPU v7x, 256 devices: a whole 4x4x8 slice. The times are simulated.
256 devices in a mesh: wave: 32 (over z, x), lev: 8 (over y, core).
Axes of the slice: x: 4, y: 4, z: 8, core: 2. Of those that a mesh axis runs over, the one named last changes fastest.
Arguments:
- legendre_values: bfloat16 [1280, 512, 1280], P(('wave', 'lev')), may hold values from -0.15625 to 0.15625
- spectra: bfloat16 [1280, 1280, 128], P(('wave', 'lev')), may hold values from -0.16699219 to 0.16699219
- wave_table: int32 [1280], replicated, may hold values from 0 to 1279, each once
- row_longitudes: int32 [512], P(('wave', 'lev')), may hold values from 20 to 5136, as said below
Outputs:
- grid_fields: float32 [512, 64, 5376], P(('wave', 'lev'))
Inputs may be any that keep to these rules, and one draw needn't show every extreme that they name: `wave_table`: every wavenumber appears in exactly one slot. `row_longitudes`: each count is 20 plus a multiple of 4; some row of every draw has 5136.
All inputs are finite; a program needn't handle non-finite values.
Results may differ from a plain program's by a relative error of at most 0.0003.
Values sent between devices are 32-bit elements; how exact they have to be, the bound alone decides.
A program may use at most 128 MiB of HBM per device.

v0:
```python
import jax
import jax.numpy as jnp
from jax import lax
from jax.sharding import PartitionSpec as P

NLON = 5376


span_width = 1024
split_width = 32


def wave_section(blocks):
    return lax.all_to_all(blocks, "wave", split_axis=1, concat_axis=0, tiled=True)


def level_section(blocks):
    return lax.all_to_all(blocks, "lev", split_axis=2, concat_axis=0, tiled=True)


def per_device(legendre_values, spectra, wave_table, row_longitudes):
    slots = legendre_values.shape[0]
    degree_count = spectra.shape[1]
    channels = spectra.shape[2]
    wave_devices = lax.axis_size("wave")
    level_devices = lax.axis_size("lev")
    block_number = lax.axis_index("wave") * level_devices + lax.axis_index("lev")
    local_waves = lax.dynamic_slice_in_dim(wave_table, block_number * slots, slots)
    degrees = jnp.arange(degree_count, dtype=jnp.int32)
    allowed = degrees[None, :] >= local_waves[:, None]
    kept = jnp.where(allowed[:, :, None], spectra, jnp.zeros_like(spectra))
    fourier = jnp.einsum("sln,snc->slc", legendre_values, kept, preferred_element_type=jnp.float32)
    local_rows = row_longitudes.shape[0]
    shaped = fourier.reshape(slots, wave_devices, level_devices, local_rows, channels)
    moved = level_section(wave_section(shaped))
    waves = wave_table.reshape(wave_devices, level_devices, slots).transpose(1, 0, 2).reshape(-1)
    total_waves = slots * wave_devices * level_devices
    moved = moved.reshape(total_waves, local_rows, channels)
    offsets = jnp.arange(span_width, dtype=jnp.int32)
    inner_steps = jnp.arange(split_width, dtype=jnp.int32)
    outer_steps = inner_steps * split_width
    base_weight = jnp.where(waves == 0, jnp.float32(1.0), jnp.float32(2.0))
    padded_width = span_width * ((NLON + span_width - 1) // span_width)

    def row_transform(items):
        coefficients, longitudes = items
        pairs = coefficients.reshape(total_waves, channels // 2, 2)
        weight = jnp.where(waves <= (longitudes - 1) // 2, base_weight, jnp.float32(0.0))
        real_part = pairs[:, :, 0] * weight[:, None]
        imag_part = pairs[:, :, 1] * weight[:, None]
        scale = jnp.float32(2.0 * jnp.pi) / longitudes.astype(jnp.float32)
        inner_angle = (waves[:, None] * inner_steps[None, :] % longitudes).astype(
            jnp.float32
        ) * scale
        outer_angle = (waves[:, None] * outer_steps[None, :] % longitudes).astype(
            jnp.float32
        ) * scale
        inner_cos = jnp.cos(inner_angle)[:, None, :]
        inner_sin = jnp.sin(inner_angle)[:, None, :]
        outer_cos = jnp.cos(outer_angle)[:, :, None]
        outer_sin = jnp.sin(outer_angle)[:, :, None]
        table_cos = (outer_cos * inner_cos - outer_sin * inner_sin).reshape(total_waves, span_width)
        table_sin = (outer_sin * inner_cos + outer_cos * inner_sin).reshape(total_waves, span_width)
        right_side = jnp.concatenate([table_cos, -table_sin], axis=0)
        block_total = (longitudes + span_width - 1) // span_width

        def add_block(lon_block, output):
            first_lon = lon_block * span_width
            turn = (waves * first_lon % longitudes).astype(jnp.float32) * scale
            cos_turn = jnp.cos(turn)[:, None]
            sin_turn = jnp.sin(turn)[:, None]
            rot_real = real_part * cos_turn - imag_part * sin_turn
            rot_imag = real_part * sin_turn + imag_part * cos_turn
            left_side = jnp.concatenate([rot_real, rot_imag], axis=0)
            piece = lax.dot_general(
                left_side, right_side, (((0,), (0,)), ((), ())), precision=lax.Precision.HIGH
            )
            piece = jnp.where(first_lon + offsets[None, :] < longitudes, piece, jnp.float32(0.0))
            return lax.dynamic_update_slice_in_dim(output, piece, first_lon, 1)

        filled = lax.fori_loop(
            0, block_total, add_block, jnp.zeros((channels // 2, padded_width), jnp.float32)
        )
        return filled[:, :NLON]

    return lax.map(row_transform, (jnp.swapaxes(moved, 0, 1), row_longitudes))


def solution(mesh):
    in_specs = (
        P(("wave", "lev"), None, None),
        P(("wave", "lev"), None, None),
        P(),
        P(("wave", "lev")),
    )
    out_specs = P(("wave", "lev"), None, None)
    return jax.shard_map(
        per_device, mesh=mesh, in_specs=in_specs, out_specs=out_specs, check_vma=False
    )
```

profile of v0, /device:TPU:8, one launch (start us, length us, event | category | flops | bytes accessed | tf_op | source)
XLA Modules:
  0.0 255.0 jit_solution(12480252689859928130)
XLA Ops:
  0.9 5.4 %fusion.42 = f32[5,512,128]{1,2,0:T(8,128)S(1)} fusion(bf16[5,512,1280]{2,1,0:T(8,128)(2,1)} %param.8, bf16[5,1280,128]{2,1,0:T(8,128)(2,1)} %param.9, pred[5,1280]{1,0:T(8,128)(4,1)S(1)} %iota_compare_fusion), kind=kOutput, calls=%fused_computation.53 | convolution fusion | flops 839680000 | bytes 9509120 | tf_op jit(solution)/shard_map/sln,snc->slc/dot_general | solution.py:32
  7.1 46.3 %all_to_all.33 = f32[5,32,8,2,128]{4,3,2,0,1:T(2,128)S(1)} all-to-all(f32[5,32,8,2,128]{4,3,2,0,1:T(2,128)S(1)} %copy.32), channel_id=1, replica_groups=mesh['wave'=32,'lev'=8] {'wave'}, dimensions={1} | all-to-all | bytes 2621440 | tf_op jit(solution)/shard_map/all_to_all | solution.py:14
  55.3 5.0 %all-to-all-start.1 = ((f32[160,1,8,2,128]{4,3,1,0,2:T(2,128)}), f32[160,1,8,2,128]{4,3,1,0,2:T(2,128)}, u32[]{:S(2)}, u32[]{:S(2)}) async-start(f32[160,1,8,2,128]{4,3,1,0,2:T(2,128)} %copy.34), calls=%async_computation.1 | async-start | bytes 2621440 | tf_op jit(solution)/shard_map/all_to_all | solution.py:18
  61.0 16.7 %all-to-all-done.1 = f32[160,1,8,2,128]{4,3,1,0,2:T(2,128)} async-done(((f32[160,1,8,2,128]{4,3,1,0,2:T(2,128)}), f32[160,1,8,2,128]{4,3,1,0,2:T(2,128)}, u32[]{:S(2)}, u32[]{:S(2)}) %all-to-all-start.1) | async-done | bytes 1310752 | tf_op jit(solution)/shard_map/all_to_all | solution.py:18
  79.2 175.8 %while.46 = (s32[]{:T(128)}, f32[2,64,5376]{2,1,0:T(8,128)}, s32[2]{0:T(128)S(1)}, f32[2,1280,128]{2,1,0:T(8,128)S(1)}, s32[1280]{0:T(1024)S(1)}, /*index=5*/f32...) while((s32[]{:T(128)}, f32[2,64,5376]{2,1,0:T(8,128)}, ...), condition=%wide.wide.region_3.4_spmd.clone, body=%wide.wide.region_0.3_spmd.clone.sunk | while | flops 1020150848 | bytes 89192168 | solution.py:86
  82.3 4.4 %fusion.59 = (f32[1280,32]{0,1:T(8,128)S(1)}, f32[1280,32]{0,1:T(8,128)S(1)}, f32[1280,32]{0,1:T(8,128)S(1)}, f32[1280,32]{0,1:T(8,128)S(1)}) fusion(f32[]{:T(128)} %div.49, s32[]{:T(128)} %select_n.190, s32[32]{0:T(128)S(1)} %iota_multiply_fusion.4, s32[1280]{0:T(1024)S(1)} %get-tuple-element.799, pred[]{:T(512)} %lt.144), kind=kLoop, calls=%fused_computation.42.clone.clone.1 | loop fusion | flops 819200 | bytes 660617 | tf_op jit(solution)/shard_map/while/body/eval_jaxpr/cos | solution.py:60
  86.6 5.5 %multiply_subtract_fusion.5 = (f32[1280,32,32]{0,2,1:T(8,128)}, f32[1280,32,32]{0,2,1:T(8,128)}) fusion(f32[1280,32]{0,1:T(8,128)S(1)} %get-tuple-element.682, f32[1280,32]{0,1:T(8,128)S(1)} %get-tuple-element.683, f32[1280,32]{0,1:T(8,128)S(1)} %get-tuple-element.684, f32[1280,32]{0,1:T(8,128)S(1)} %get-tuple-element.685), kind=kLoop, calls=%fused_computation.21.clone.clone.1 | loop fusion | flops 9175040 | bytes 11141120 | tf_op jit(solution)/shard_map/while/body/eval_jaxpr/sub | solution.py:62
  92.1 9.1 %pad_maximum_fusion.3 = f32[2560,1024]{0,1:T(8,128)} fusion(f32[1280,1024]{0,1:T(8,128)} %bitcast.49, f32[1280,1024]{0,1:T(8,128)} %bitcast.48), kind=kLoop, calls=%fused_computation.19.clone.clone.1 | loop fusion | flops 2621440 | bytes 20971520 | tf_op jit(solution)/shard_map/while/body/eval_jaxpr/concatenate | solution.py:64
  101.2 11.4 %copy.61 = f32[2560,1024]{1,0:T(8,128)} copy(f32[2560,1024]{0,1:T(8,128)} %pad_maximum_fusion.3) | data formatting | bytes 20971520 | tf_op jit(solution)/shard_map/while/body/eval_jaxpr/while | solution.py:81
  117.0 47.6 %while.47 = (s32[]{:T(128)}, f32[64,6144]{1,0:T(8,128)}, s32[]{:T(128)}, s32[1024]{0:T(1024)S(1)}, s32[]{:T(128)}, /*index=5*/s32[1280]{0:T(1024)S(1)}, s32[]{:T...) while((s32[]{:T(128)}, f32[64,6144]{1,0:T(8,128)}, ...), condition=%wide.region_2.2_spmd, body=%wide.region_1.1_spmd.sunk | while | flops 1007368704 | bytes 12745948 | solution.py:81
  118.3 8.2 %fusion.63 = f32[64,6144]{1,0:T(8,128)} fusion(f32[64,6144]{1,0:T(8,128)} %get-tuple-element.723, s32[]{:T(128)S(6)} %select_n.194, f32[2560,1024]{1,0:T(8,128)} %get-tuple-element.749, f32[1280,64]{1,0:T(8,128)S(1)} %get-tuple-element.704, f32[1280,64]{1,0:T(8,128)S(1)} %get-tuple-element.705, pred[1024]{0:T(1024)(128)(4,1)S(1)} %add_compare_fusion.2), kind=kOutput, calls=%fused_computation.8.clone.1 | convolution fusion | flops 1006862336 | bytes 11404292 | tf_op jit(solution)/shard_map/while/body/eval_jaxpr/while/body/dot_general | solution.py:75
  127.9 8.2 %fusion.63 = f32[64,6144]{1,0:T(8,128)} fusion(f32[64,6144]{1,0:T(8,128)} %get-tuple-element.723, s32[]{:T(128)S(6)} %select_n.194, f32[2560,1024]{1,0:T(8,128)} %get-tuple-element.749, f32[1280,64]{1,0:T(8,128)S(1)} %get-tuple-element.704, f32[1280,64]{1,0:T(8,128)S(1)} %get-tuple-element.705, pred[1024]{0:T(1024)(128)(4,1)S(1)} %add_compare_fusion.2), kind=kOutput, calls=%fused_computation.8.clone.1 | convolution fusion | flops 1006862336 | bytes 11404292 | tf_op jit(solution)/shard_map/while/body/eval_jaxpr/while/body/dot_general | solution.py:75
  137.4 8.2 %fusion.63 = f32[64,6144]{1,0:T(8,128)} fusion(f32[64,6144]{1,0:T(8,128)} %get-tuple-element.723, s32[]{:T(128)S(6)} %select_n.194, f32[2560,1024]{1,0:T(8,128)} %get-tuple-element.749, f32[1280,64]{1,0:T(8,128)S(1)} %get-tuple-element.704, f32[1280,64]{1,0:T(8,128)S(1)} %get-tuple-element.705, pred[1024]{0:T(1024)(128)(4,1)S(1)} %add_compare_fusion.2), kind=kOutput, calls=%fused_computation.8.clone.1 | convolution fusion | flops 1006862336 | bytes 11404292 | tf_op jit(solution)/shard_map/while/body/eval_jaxpr/while/body/dot_general | solution.py:75
  146.9 8.2 %fusion.63 = f32[64,6144]{1,0:T(8,128)} fusion(f32[64,6144]{1,0:T(8,128)} %get-tuple-element.723, s32[]{:T(128)S(6)} %select_n.194, f32[2560,1024]{1,0:T(8,128)} %get-tuple-element.749, f32[1280,64]{1,0:T(8,128)S(1)} %get-tuple-element.704, f32[1280,64]{1,0:T(8,128)S(1)} %get-tuple-element.705, pred[1024]{0:T(1024)(128)(4,1)S(1)} %add_compare_fusion.2), kind=kOutput, calls=%fused_computation.8.clone.1 | convolution fusion | flops 1006862336 | bytes 11404292 | tf_op jit(solution)/shard_map/while/body/eval_jaxpr/while/body/dot_general | solution.py:75
  156.4 8.2 %fusion.63 = f32[64,6144]{1,0:T(8,128)} fusion(f32[64,6144]{1,0:T(8,128)} %get-tuple-element.723, s32[]{:T(128)S(6)} %select_n.194, f32[2560,1024]{1,0:T(8,128)} %get-tuple-element.749, f32[1280,64]{1,0:T(8,128)S(1)} %get-tuple-element.704, f32[1280,64]{1,0:T(8,128)S(1)} %get-tuple-element.705, pred[1024]{0:T(1024)(128)(4,1)S(1)} %add_compare_fusion.2), kind=kOutput, calls=%fused_computation.8.clone.1 | convolution fusion | flops 1006862336 | bytes 11404292 | tf_op jit(solution)/shard_map/while/body/eval_jaxpr/while/body/dot_general | solution.py:75
  174.4 5.5 %multiply_subtract_fusion.5 = (f32[1280,32,32]{0,2,1:T(8,128)}, f32[1280,32,32]{0,2,1:T(8,128)}) fusion(f32[1280,32]{0,1:T(8,128)S(1)} %get-tuple-element.682, f32[1280,32]{0,1:T(8,128)S(1)} %get-tuple-element.683, f32[1280,32]{0,1:T(8,128)S(1)} %get-tuple-element.684, f32[1280,32]{0,1:T(8,128)S(1)} %get-tuple-element.685), kind=kLoop, calls=%fused_computation.21.clone.clone.1 | loop fusion | flops 9175040 | bytes 11141120 | tf_op jit(solution)/shard_map/while/body/eval_jaxpr/sub | solution.py:62
  179.9 9.1 %pad_maximum_fusion.3 = f32[2560,1024]{0,1:T(8,128)} fusion(f32[1280,1024]{0,1:T(8,128)} %bitcast.49, f32[1280,1024]{0,1:T(8,128)} %bitcast.48), kind=kLoop, calls=%fused_computation.19.clone.clone.1 | loop fusion | flops 2621440 | bytes 20971520 | tf_op jit(solution)/shard_map/while/body/eval_jaxpr/concatenate | solution.py:64
  189.0 11.4 %copy.61 = f32[2560,1024]{1,0:T(8,128)} copy(f32[2560,1024]{0,1:T(8,128)} %pad_maximum_fusion.3) | data formatting | bytes 20971520 | tf_op jit(solution)/shard_map/while/body/eval_jaxpr/while | solution.py:81
  204.8 47.6 %while.47 = (s32[]{:T(128)}, f32[64,6144]{1,0:T(8,128)}, s32[]{:T(128)}, s32[1024]{0:T(1024)S(1)}, s32[]{:T(128)}, /*index=5*/s32[1280]{0:T(1024)S(1)}, s32[]{:T...) while((s32[]{:T(128)}, f32[64,6144]{1,0:T(8,128)}, ...), condition=%wide.region_2.2_spmd, body=%wide.region_1.1_spmd.sunk | while | flops 1007368704 | bytes 12745948 | solution.py:81
  206.1 8.2 %fusion.63 = f32[64,6144]{1,0:T(8,128)} fusion(f32[64,6144]{1,0:T(8,128)} %get-tuple-element.723, s32[]{:T(128)S(6)} %select_n.194, f32[2560,1024]{1,0:T(8,128)} %get-tuple-element.749, f32[1280,64]{1,0:T(8,128)S(1)} %get-tuple-element.704, f32[1280,64]{1,0:T(8,128)S(1)} %get-tuple-element.705, pred[1024]{0:T(1024)(128)(4,1)S(1)} %add_compare_fusion.2), kind=kOutput, calls=%fused_computation.8.clone.1 | convolution fusion | flops 1006862336 | bytes 11404292 | tf_op jit(solution)/shard_map/while/body/eval_jaxpr/while/body/dot_general | solution.py:75
  215.7 8.2 %fusion.63 = f32[64,6144]{1,0:T(8,128)} fusion(f32[64,6144]{1,0:T(8,128)} %get-tuple-element.723, s32[]{:T(128)S(6)} %select_n.194, f32[2560,1024]{1,0:T(8,128)} %get-tuple-element.749, f32[1280,64]{1,0:T(8,128)S(1)} %get-tuple-element.704, f32[1280,64]{1,0:T(8,128)S(1)} %get-tuple-element.705, pred[1024]{0:T(1024)(128)(4,1)S(1)} %add_compare_fusion.2), kind=kOutput, calls=%fused_computation.8.clone.1 | convolution fusion | flops 1006862336 | bytes 11404292 | tf_op jit(solution)/shard_map/while/body/eval_jaxpr/while/body/dot_general | solution.py:75
  225.2 8.2 %fusion.63 = f32[64,6144]{1,0:T(8,128)} fusion(f32[64,6144]{1,0:T(8,128)} %get-tuple-element.723, s32[]{:T(128)S(6)} %select_n.194, f32[2560,1024]{1,0:T(8,128)} %get-tuple-element.749, f32[1280,64]{1,0:T(8,128)S(1)} %get-tuple-element.704, f32[1280,64]{1,0:T(8,128)S(1)} %get-tuple-element.705, pred[1024]{0:T(1024)(128)(4,1)S(1)} %add_compare_fusion.2), kind=kOutput, calls=%fused_computation.8.clone.1 | convolution fusion | flops 1006862336 | bytes 11404292 | tf_op jit(solution)/shard_map/while/body/eval_jaxpr/while/body/dot_general | solution.py:75
  234.7 8.2 %fusion.63 = f32[64,6144]{1,0:T(8,128)} fusion(f32[64,6144]{1,0:T(8,128)} %get-tuple-element.723, s32[]{:T(128)S(6)} %select_n.194, f32[2560,1024]{1,0:T(8,128)} %get-tuple-element.749, f32[1280,64]{1,0:T(8,128)S(1)} %get-tuple-element.704, f32[1280,64]{1,0:T(8,128)S(1)} %get-tuple-element.705, pred[1024]{0:T(1024)(128)(4,1)S(1)} %add_compare_fusion.2), kind=kOutput, calls=%fused_computation.8.clone.1 | convolution fusion | flops 1006862336 | bytes 11404292 | tf_op jit(solution)/shard_map/while/body/eval_jaxpr/while/body/dot_general | solution.py:75
  244.2 8.2 %fusion.63 = f32[64,6144]{1,0:T(8,128)} fusion(f32[64,6144]{1,0:T(8,128)} %get-tuple-element.723, s32[]{:T(128)S(6)} %select_n.194, f32[2560,1024]{1,0:T(8,128)} %get-tuple-element.749, f32[1280,64]{1,0:T(8,128)S(1)} %get-tuple-element.704, f32[1280,64]{1,0:T(8,128)S(1)} %get-tuple-element.705, pred[1024]{0:T(1024)(128)(4,1)S(1)} %add_compare_fusion.2), kind=kOutput, calls=%fused_computation.8.clone.1 | convolution fusion | flops 1006862336 | bytes 11404292 | tf_op jit(solution)/shard_map/while/body/eval_jaxpr/while/body/dot_general | solution.py:75
  (84 shorter events, 35.3 us)
Async XLA Ops:
  53.5 6.8 %copy-start.3 = (s32[1280]{0:T(1024)S(1)}, s32[1280]{0:T(1024)}, u32[]{:S(2)}) copy-start(s32[1280]{0:T(1024)} %param.10) | copy-start | bytes 15364
  55.3 23.9 %copy-start.4 = (s32[2]{0:T(128)S(1)}, s32[2]{0:T(128)}, u32[]{:S(2)}) copy-start(s32[2]{0:T(128)} %param.11) | copy-start | bytes 28
  55.3 22.5 %all-to-all-start.1 = ((f32[160,1,8,2,128]{4,3,1,0,2:T(2,128)}), f32[160,1,8,2,128]{4,3,1,0,2:T(2,128)}, u32[]{:S(2)}, u32[]{:S(2)}) async-start(f32[160,1,8,2,128]{4,3,1,0,2:T(2,128)} %copy.34), calls=%async_computation.1 | async-start | bytes 2621440 | tf_op jit(solution)/shard_map/all_to_all | solution.py:18
  60.5 18.6 %copy-start.2 = (s32[8,32,5]{2,1,0:T(8,128)}, s32[8,32,5]{2,1,0:T(8,128)S(1)}, u32[]{:S(2)}) copy-start(s32[8,32,5]{2,1,0:T(8,128)S(1)} %copy.36) | copy-start | bytes 15364
  79.4 33.9 %copy-start = (f32[2,1280,128]{2,1,0:T(8,128)}, f32[2,1280,128]{2,1,0:T(8,128)S(1)}, u32[]{:S(2)}) copy-start(f32[2,1280,128]{2,1,0:T(8,128)S(1)} %get-tuple-element.795) | copy-start | bytes 3932164 | tf_op jit(solution)/shard_map/while
  164.6 2.6 %copy-start.1 = (f32[2,1280,128]{2,1,0:T(8,128)S(1)}, f32[2,1280,128]{2,1,0:T(8,128)}, u32[]{:S(2)}) copy-start(f32[2,1280,128]{2,1,0:T(8,128)} %copy-done) | copy-start | bytes 3932164 | tf_op jit(solution)/shard_map/while
  167.2 33.8 %copy-start = (f32[2,1280,128]{2,1,0:T(8,128)}, f32[2,1280,128]{2,1,0:T(8,128)S(1)}, u32[]{:S(2)}) copy-start(f32[2,1280,128]{2,1,0:T(8,128)S(1)} %get-tuple-element.795) | copy-start | bytes 3932164 | tf_op jit(solution)/shard_map/while
  252.4 2.6 %copy-start.1 = (f32[2,1280,128]{2,1,0:T(8,128)S(1)}, f32[2,1280,128]{2,1,0:T(8,128)}, u32[]{:S(2)}) copy-start(f32[2,1280,128]{2,1,0:T(8,128)} %copy-done) | copy-start | bytes 3932164 | tf_op jit(solution)/shard_map/while
where the time goes:
time: 256 us; the launch traced here: 255 us
  matrix products  87.7 us (34%)
  other arithmetic  50.7 us (20%)
  blocking collectives  46.3 us (18%)
  local copies, waits for them, and re-layouts  40.8 us (16%)
  waiting for transfers between devices  16.7 us (7%)
  loops' own time  7.63 us (3%)
  starting transfers between devices  5.05 us (2%)
    dot_general x10, matrix products, add_block(): lax.dot_general(left_side, right_side, (((0,), (0,)), ((), ())), precisio...  82.3 us
    all_to_all x1, blocking collectives, wave_section(): lax.all_to_all(blocks, 'wave', split_axis=1, concat_axis=0, tiled=True)  46.3 us
    while x6, local copies, waits for them, and re-layouts, row_transform(): lax.fori_loop(0, block_total, add_block, jnp.zeros((channels // 2, padded...  23.7 us
    concatenate x2, other arithmetic, row_transform(): right_side = jnp.concatenate([table_cos, -table_sin], axis=0)  18.1 us
    all_to_all x1, waiting for transfers between devices, level_section(): lax.all_to_all(blocks, 'lev', split_axis=2, concat_axis=0, tiled=True)  16.7 us
    sub x2, other arithmetic, row_transform(): outer_cos * inner_cos - outer_sin * inner_sin  11 us
    cos x2, other arithmetic, row_transform(): outer_cos = jnp.cos(outer_angle)[:, :, None]  8.73 us
    another operation x1, loops' own time, per_device(): return lax.map(row_transform, (jnp.swapaxes(moved, 0, 1), row_longitudes))  7.41 us
  transfers between devices with their start and end apart: 1, of which 1 were waited for; matrix products, arithmetic and copies ran while one was open for 0% of the time, Pallas kernels for 0%

commit v1 on v0

v1 whole, which is shorter than its diff:
```python
import functools

import jax
import jax.numpy as jnp
from jax import lax
from jax.experimental import pallas as pl
from jax.experimental.pallas import tpu as pltpu
from jax.sharding import PartitionSpec as P

MESH = pl.DeviceIdType.MESH

SLOTS = 5
DEGREES = 1280
ROWS = 512
CHANNELS = 128
FIELDS = 64
LOCAL_ROWS = 2
DEVICES = 256
NLON = 5376
HALF = 256
SPAN = 2 * HALF
BLOCKS = 11
STACKED = BLOCKS * FIELDS

COS_TERMS = (
    0.9999999996168156,
    -19.73920863354667,
    64.93938183835107,
    -85.4564814603686,
    60.24009011425828,
    -26.392650988301078,
    7.765225095262238,
    -1.4134373617596543,
)
SIN_TERMS = (
    6.283185293777215,
    -41.341697721207424,
    81.605000209223,
    -76.70070302960839,
    42.00769493017941,
    -14.834123486306066,
    3.1498534224128543,
)


def horner(terms, square):
    total = jnp.full_like(square, terms[-1])
    for term in terms[-2::-1]:
        total = total * square + jnp.float32(term)
    return total


def cos_sin_of_turns(product, period, inverse):
    whole = jnp.round(product * inverse)
    turn = (product - whole * period) * inverse
    square = turn * turn
    return horner(COS_TERMS, square), turn * horner(SIN_TERMS, square)


def split(values):
    high = values.astype(jnp.bfloat16)
    low = (values - high.astype(jnp.float32)).astype(jnp.bfloat16)
    return high, low


def legendre_sums(wave_table, legendre_values, spectra):
    me = lax.axis_index("wave") * lax.axis_size("lev") + lax.axis_index("lev")
    wavenumbers = lax.dynamic_slice_in_dim(wave_table, me * SLOTS, SLOTS)
    degrees = jnp.arange(DEGREES, dtype=jnp.int32)
    allowed = degrees[None, :] >= wavenumbers[:, None]
    kept = jnp.where(allowed[:, :, None], spectra, jnp.zeros_like(spectra))
    return jnp.einsum("srn,snc->src", legendre_values, kept, preferred_element_type=jnp.float32)


def exchange(wave_table, legendre_values, spectra):
    fourier = legendre_sums(wave_table, legendre_values, spectra)
    moved = lax.all_to_all(fourier, ("wave", "lev"), split_axis=1, concat_axis=1, tiled=True)
    return jnp.swapaxes(moved.reshape(SLOTS, DEVICES, LOCAL_ROWS, CHANNELS), 1, 2)


def rows_kernel(longitudes_ref, waves_ref, arrived_ref, out_ref, turned, cos_sum, sin_sum):
    longitudes = longitudes_ref[pl.program_id(0)]
    period = (2 * longitudes).astype(jnp.float32)
    period_row = jnp.full((8, 128), period, jnp.float32)
    inverse = (jnp.float32(1.0) / period_row)[:1, :1]
    largest = lax.div(longitudes - 1, 2).astype(jnp.float32)
    odd = (2 * lax.broadcasted_iota(jnp.int32, (HALF, HALF), 1) + 1).astype(jnp.float32)
    centre = (
        2 * SPAN * lax.broadcasted_iota(jnp.int32, (16, HALF), 0) + (SPAN - 1)
    ).astype(jnp.float32)
    cos_sum[...] = jnp.zeros_like(cos_sum)
    sin_sum[...] = jnp.zeros_like(sin_sum)

    def slot_step(slot, carry):
        wave_row = waves_ref[pl.ds(slot, 1), :].astype(jnp.float32)
        wave_column = jnp.broadcast_to(wave_row, (HALF, HALF)).T
        table_cos, table_sin = cos_sin_of_turns(wave_column * odd, period, inverse)
        cos_high, cos_low = split(table_cos)
        sin_high, sin_low = split(table_sin)
        cos_table = jnp.concatenate([cos_high, cos_high, cos_low], axis=0)
        sin_table = jnp.concatenate([sin_high, sin_high, sin_low], axis=0)
        block_cos, block_sin = cos_sin_of_turns(wave_row * centre, period, inverse)
        weight = jnp.where(
            wave_row > largest,
            jnp.float32(0.0),
            jnp.where(wave_row == 0, jnp.float32(1.0), jnp.float32(2.0)),
        )
        for half in range(2):
            turned[half] = arrived_ref[slot, 0, pl.ds(half * 128, 128), :].T
        real, imag = (
            jnp.concatenate(
                [turned[half, pl.ds(part, FIELDS, stride=2), :] for half in range(2)], axis=1
            )
            * weight
            for part in range(2)
        )
        real_parts = []
        imag_parts = []
        for k in range(BLOCKS):
            c = block_cos[k : k + 1, :]
            s = block_sin[k : k + 1, :]
            high, low = split(real * c - imag * s)
            real_parts.append(jnp.concatenate([high, low, high], axis=1))
            high, low = split(real * s + imag * c)
            imag_parts.append(jnp.concatenate([high, low, high], axis=1))
        real_side = jnp.concatenate(real_parts, axis=0)
        imag_side = jnp.concatenate(imag_parts, axis=0)
        cos_sum[...] += jnp.dot(real_side, cos_table, preferred_element_type=jnp.float32)
        sin_sum[...] += jnp.dot(imag_side, sin_table, preferred_element_type=jnp.float32)
        return carry

    lax.fori_loop(0, SLOTS, slot_step, 0)
    backwards = 127 - lax.broadcasted_iota(jnp.int32, (FIELDS, 128), 1)
    column = lax.broadcasted_iota(jnp.int32, (FIELDS, 128), 1)
    for k in range(BLOCKS):
        rows = pl.ds(k * FIELDS, FIELDS)
        for part in range(2):
            lanes = pl.ds(part * 128, 128)
            c = cos_sum[rows, lanes]
            s = sin_sum[rows, lanes]
            first = k * SPAN + 128 * (1 - part)
            values = jnp.take_along_axis(c + s, backwards, axis=1)
            out_ref[0, :, pl.ds(first, 128)] = jnp.where(
                column + first < longitudes, values, jnp.float32(0.0)
            )
            first = k * SPAN + HALF + 128 * part
            if first < NLON:
                out_ref[0, :, pl.ds(first, 128)] = jnp.where(
                    column + first < longitudes, c - s, jnp.float32(0.0)
                )


def rows_transform(row_longitudes, waves, arrived, interpret=False):
    return pl.pallas_call(
        rows_kernel,
        out_shape=jax.ShapeDtypeStruct((LOCAL_ROWS, FIELDS, NLON), jnp.float32),
        grid=(LOCAL_ROWS,),
        in_specs=[
            pl.BlockSpec(memory_space=pltpu.SMEM),
            pl.BlockSpec(memory_space=pltpu.VMEM),
            pl.BlockSpec((SLOTS, 1, DEVICES, CHANNELS), lambda r: (0, r, 0, 0)),
        ],
        out_specs=pl.BlockSpec((1, FIELDS, NLON), lambda r: (r, 0, 0)),
        scratch_shapes=[
            pltpu.VMEM((2, CHANNELS, 128), jnp.float32),
            pltpu.VMEM((STACKED, HALF), jnp.float32),
            pltpu.VMEM((STACKED, HALF), jnp.float32),
        ],
        compiler_params=pltpu.CompilerParams(vmem_limit_bytes=40 << 20),
        interpret=interpret,
    )(row_longitudes, waves, arrived)


def per_device(legendre_values, spectra, wave_table, row_longitudes):
    waves = wave_table.reshape(DEVICES, SLOTS).T
    arrived = exchange(wave_table, legendre_values, spectra)
    return rows_transform(row_longitudes, waves, arrived)


def solution(mesh):
    in_specs = (
        P(("wave", "lev"), None, None),
        P(("wave", "lev"), None, None),
        P(),
        P(("wave", "lev")),
    )
    out_specs = P(("wave", "lev"), None, None)
    return jax.shard_map(
        per_device, mesh=mesh, in_specs=in_specs, out_specs=out_specs, check_vma=False
    )
```

time: 256 us -> 91.5 us (0.36)
  the two profiles are of different devices: /device:TPU:8 before, /device:TPU:1 now
where the time goes in v1:
time: 91.5 us; the launch traced here: 91.2 us
  waiting for transfers between devices  52.8 us (58%)
  starting transfers between devices  15.7 us (17%)
  Pallas kernels  13.9 us (15%)
  matrix products  5.36 us (6%)
  local copies, waits for them, and re-layouts  3.47 us (4%)
    all_to_all x1, waiting for transfers between devices, exchange(): lax.all_to_all(fourier, ('wave', 'lev'), split_axis=1, concat_axis=1, til...  52.8 us
    all_to_all x1, starting transfers between devices, exchange(): lax.all_to_all(fourier, ('wave', 'lev'), split_axis=1, concat_axis=1, til...  15.7 us
    pallas_call x1, Pallas kernels, rows_transform(): pl.pallas_call(rows_kernel, out_shape=jax.ShapeDtypeStruct((LOCAL_ROWS, F...  13.9 us
    dot_general x1, matrix products, legendre_sums(): jnp.einsum('srn,snc->src', legendre_values, kept, preferred_element_type=...  5.36 us
  transfers between devices with their start and end apart: 1, of which 1 were waited for; matrix products, arithmetic and copies ran while one was open for 0% of the time, Pallas kernels for 0%

profile of v1, /device:TPU:1, one launch (start us, length us, event | category | flops | bytes accessed | tf_op | source)
XLA Modules:
  0.0 91.2 jit_solution(5873034104381520607)
XLA Ops:
  0.0 0.8 dynamic_slice.3
  0.8 0.1 iota_compare_fusion
  0.9 5.4 %fusion.3 = f32[5,512,128]{1,2,0:T(8,128)S(1)} fusion(bf16[5,512,1280]{2,1,0:T(8,128)(2,1)} %param.4, bf16[5,1280,128]{2,1,0:T(8,128)(2,1)} %param.5, pred[5,1280]{1,0:T(8,128)(4,1)S(1)} %iota_compare_fusion), kind=kOutput, calls=%fused_computation.3 | convolution fusion | flops 839680000 | bytes 9509120 | tf_op jit(solution)/shard_map/srn,snc->src/dot_general | solution.py:72
  6.2 1.8 %copy.12 = f32[5,512,128]{2,0,1:T(8,128)} copy(f32[5,512,128]{1,2,0:T(8,128)S(1)} %fusion.3) | data formatting | bytes 2621440 | tf_op jit(solution)/shard_map/srn,snc->src/dot_general | solution.py:72
  8.0 0.0 copy-start.1
  8.0 15.7 %all-to-all-start = ((f32[5,512,128]{2,0,1:T(8,128)}), f32[5,512,128]{2,0,1:T(8,128)S(1)}, u32[]{:S(2)}, u32[]{:S(2)}) async-start(f32[5,512,128]{2,0,1:T(8,128)} %copy.12), calls=%async_computation | async-start | bytes 4194304 | tf_op jit(solution)/shard_map/all_to_all | solution.py:77
  23.7 0.0 copy-done.1
  23.7 0.2 reshape.27
  23.9 0.1 copy.10
  23.9 52.8 %all-to-all-done = f32[5,512,128]{2,0,1:T(8,128)S(1)} async-done(((f32[5,512,128]{2,0,1:T(8,128)}), f32[5,512,128]{2,0,1:T(8,128)S(1)}, u32[]{:S(2)}, u32[]{:S(2)}) %all-to-all-start) | async-done | bytes 1310752 | tf_op jit(solution)/shard_map/all_to_all | solution.py:77
  76.7 0.0 copy-start
  76.7 0.4 copy.19
  77.1 0.2 copy-done
  77.3 13.9 %shard_map.46 = f32[2,64,5376]{2,1,0:T(8,128)} custom-call(s32[2]{0:T(128)S(1)} %copy-done, s32[5,256]{1,0:T(8,128)S(1)} %bitcast.9, f32[5,2,256,128]{3,2,1,0:T(8,128)S(1)} %bitcast.8), custom_call_target="tpu_custom_call" | custom-call | tf_op jit(solution)/shard_map/pallas_call | solution.py:154
Async XLA Ops:
  8.0 15.7 %copy-start.1 = (s32[1280]{0:T(1024)S(1)}, s32[1280]{0:T(1024)}, u32[]{:S(2)}) copy-start(s32[1280]{0:T(1024)} %param.6) | copy-start | bytes 15364
  8.0 68.7 %all-to-all-start = ((f32[5,512,128]{2,0,1:T(8,128)}), f32[5,512,128]{2,0,1:T(8,128)S(1)}, u32[]{:S(2)}, u32[]{:S(2)}) async-start(f32[5,512,128]{2,0,1:T(8,128)} %copy.12), calls=%async_computation | async-start | bytes 4194304 | tf_op jit(solution)/shard_map/all_to_all | solution.py:77
  76.7 0.7 copy-start

commit v2 on v1

--- a/solution.py
+++ b/solution.py
@@ -15,7 +15,11 @@
 CHANNELS = 128
 FIELDS = 64
 LOCAL_ROWS = 2
-DEVICES = 256
+PLANES = 8
+PER_PLANE = 4
+WAVES = PLANES * PER_PLANE
+LEVS = 8
+DEVICES = WAVES * LEVS
 NLON = 5376
 HALF = 256
 SPAN = 2 * HALF
@@ -63,19 +67,158 @@
     return high, low
 
 
-def legendre_sums(wave_table, legendre_values, spectra):
-    me = lax.axis_index("wave") * lax.axis_size("lev") + lax.axis_index("lev")
-    wavenumbers = lax.dynamic_slice_in_dim(wave_table, me * SLOTS, SLOTS)
-    degrees = jnp.arange(DEGREES, dtype=jnp.int32)
-    allowed = degrees[None, :] >= wavenumbers[:, None]
-    kept = jnp.where(allowed[:, :, None], spectra, jnp.zeros_like(spectra))
-    return jnp.einsum("srn,snc->src", legendre_values, kept, preferred_element_type=jnp.float32)
+def exchange_kernel(
+    table_ref, legendre_ref, spectra_ref, out_ref,
+    legendre, spectra, fourier, by_lev, by_x, by_z,
+    load_sem, send_sem, lev_sem, x_sem, z_sem, own_sem, out_sem,
+):
+    wave = lax.axis_index("wave")
+    lev = lax.axis_index("lev")
+    z, x = lax.div(wave, PER_PLANE), lax.rem(wave, PER_PLANE)
+    me = wave * LEVS + lev
+    lev_peers = [lax.rem(lev + k, LEVS) for k in range(1, LEVS)]
+    x_peers = [lax.rem(x + k, PER_PLANE) for k in range(1, PER_PLANE)]
+    z_peers = [lax.rem(z + k, PLANES) for k in (4, 3, 5, 2, 6, 1, 7)]
+
+    def load(slot):
+        return (
+            pltpu.make_async_copy(spectra_ref.at[slot], spectra.at[slot], load_sem.at[0, slot]),
+            pltpu.make_async_copy(legendre_ref.at[slot], legendre.at[slot], load_sem.at[1, slot]),
+        )
+
+    for slot in range(SLOTS):
+        for copy in load(slot):
+            copy.start()
+
+    barrier = pltpu.get_barrier_semaphore()
+    for peer in z_peers:
+        pl.semaphore_signal(
+            barrier, inc=1, device_id=(peer * PER_PLANE + x, lev), device_id_type=MESH
+        )
+    for peer in x_peers:
+        pl.semaphore_signal(
+            barrier, inc=1, device_id=(z * PER_PLANE + peer, lev), device_id_type=MESH
+        )
+    for peer in lev_peers:
+        pl.semaphore_signal(barrier, inc=1, device_id=(wave, peer), device_id_type=MESH)
+
+    degree = lax.broadcasted_iota(jnp.int32, (DEGREES, CHANNELS), 0)
+
+    def legendre_step(slot):
+        for copy in load(slot):
+            copy.wait()
+        wavenumber = table_ref[me * SLOTS + slot]
+        values = spectra[slot].astype(jnp.float32)
+        kept = jnp.where(degree >= wavenumber, values, jnp.float32(0.0)).astype(jnp.bfloat16)
+        sums = jnp.dot(legendre[slot], kept, preferred_element_type=jnp.float32)
+        fourier[slot] = sums.reshape(WAVES, LEVS * LOCAL_ROWS, CHANNELS)
+
+    def move(source, target, peers, own, where, stage, slot, recv):
+        for peer in peers:
+            pltpu.make_async_remote_copy(
+                src_ref=source(peer),
+                dst_ref=target,
+                send_sem=send_sem.at[stage],
+                recv_sem=recv.at[slot],
+                device_id=where(peer),
+                device_id_type=MESH,
+            ).start()
+        pltpu.make_async_copy(source(own), target, own_sem.at[stage, slot]).start()
+
+    def move_lev(slot):
+        move(
+            lambda peer: fourier.at[slot, :, pl.ds(peer * LOCAL_ROWS, LOCAL_ROWS), :],
+            by_lev.at[slot, :, :, lev, :],
+            lev_peers, lev, lambda peer: (wave, peer), 0, slot, lev_sem,
+        )
+
+    def move_x(slot):
+        move(
+            lambda peer: by_lev.at[slot].reshape(
+                PLANES, PER_PLANE, LOCAL_ROWS, LEVS, CHANNELS
+            ).at[:, peer],
+            by_x.at[slot, :, :, x],
+            x_peers, x, lambda peer: (z * PER_PLANE + peer, lev), 1, slot, x_sem,
+        )
+
+    def move_z(slot):
+        move(
+            lambda peer: by_x.at[slot, peer],
+            by_z.at[slot, :, z],
+            z_peers, z, lambda peer: (peer * PER_PLANE + x, lev), 2, slot, z_sem,
+        )
+
+    def arrived(source, target, region, stage, slot, recv):
+        pltpu.make_async_copy(region, region, recv.at[slot]).wait()
+        pltpu.make_async_copy(source, target, own_sem.at[stage, slot]).wait()
+
+    def lev_arrived(slot):
+        arrived(
+            fourier.at[slot, :, pl.ds(0, LOCAL_ROWS), :], by_lev.at[slot, :, :, 0, :],
+            by_lev.at[slot, pl.ds(0, 28)], 0, slot, lev_sem,
+        )
+
+    def x_arrived(slot):
+        arrived(
+            by_x.at[slot, :, :, 0], by_x.at[slot, :, :, 0],
+            by_x.at[slot, pl.ds(0, 6)], 1, slot, x_sem,
+        )
+
+    def z_arrived(slot):
+        arrived(
+            by_x.at[slot, 0], by_z.at[slot, :, 0],
+            by_z.at[slot, :, pl.ds(0, 7)], 2, slot, z_sem,
+        )
+
+    legendre_step(0)
+    pl.semaphore_wait(barrier, LEVS + PER_PLANE + PLANES - 3)
+    move_lev(0)
+    for slot in range(1, SLOTS):
+        legendre_step(slot)
+        move_lev(slot)
+    for turn in range(SLOTS + 1):
+        if turn < SLOTS:
+            lev_arrived(turn)
+            move_x(turn)
+        if turn >= 1:
+            x_arrived(turn - 1)
+            move_z(turn - 1)
+    for slot in range(SLOTS):
+        z_arrived(slot)
+        pltpu.make_async_copy(by_z.at[slot], out_ref.at[slot], out_sem).start()
+    pltpu.make_async_copy(by_lev.at[:, pl.ds(0, 28)], by_lev.at[:, pl.ds(0, 28)], send_sem.at[0]).wait()
+    pltpu.make_async_copy(by_x.at[:, pl.ds(0, 6)], by_x.at[:, pl.ds(0, 6)], send_sem.at[1]).wait()
+    pltpu.make_async_copy(by_x.at[:, pl.ds(0, 7)], by_x.at[:, pl.ds(0, 7)], send_sem.at[2]).wait()
+    pltpu.make_async_copy(by_z, out_ref, out_sem).wait()
 
 
 def exchange(wave_table, legendre_values, spectra):
-    fourier = legendre_sums(wave_table, legendre_values, spectra)
-    moved = lax.all_to_all(fourier, ("wave", "lev"), split_axis=1, concat_axis=1, tiled=True)
-    return jnp.swapaxes(moved.reshape(SLOTS, DEVICES, LOCAL_ROWS, CHANNELS), 1, 2)
+    any_space = pl.BlockSpec(memory_space=pl.ANY)
+    final = (SLOTS, LOCAL_ROWS, PLANES, PER_PLANE, LEVS, CHANNELS)
+    return pl.pallas_call(
+        exchange_kernel,
+        out_shape=jax.ShapeDtypeStruct(final, jnp.float32),
+        in_specs=[pl.BlockSpec(memory_space=pltpu.SMEM), any_space, any_space],
+        out_specs=any_space,
+        scratch_shapes=[
+            pltpu.VMEM((SLOTS, ROWS, DEGREES), jnp.bfloat16),
+            pltpu.VMEM((SLOTS, DEGREES, CHANNELS), jnp.bfloat16),
+            pltpu.VMEM((SLOTS, WAVES, LEVS * LOCAL_ROWS, CHANNELS), jnp.float32),
+            pltpu.VMEM((SLOTS, WAVES, LOCAL_ROWS, LEVS, CHANNELS), jnp.float32),
+            pltpu.VMEM((SLOTS, PLANES, LOCAL_ROWS, PER_PLANE, LEVS, CHANNELS), jnp.float32),
+            pltpu.VMEM(final, jnp.float32),
+            pltpu.SemaphoreType.DMA((2, SLOTS)),
+            pltpu.SemaphoreType.DMA((3,)),
+            pltpu.SemaphoreType.DMA((SLOTS,)),
+            pltpu.SemaphoreType.DMA((SLOTS,)),
+            pltpu.SemaphoreType.DMA((SLOTS,)),
+            pltpu.SemaphoreType.DMA((3, SLOTS)),
+            pltpu.SemaphoreType.DMA,
+        ],
+        compiler_params=pltpu.CompilerParams(
+            collective_id=0, has_side_effects=True, vmem_limit_bytes=60 << 20
+        ),
+    )(wave_table, legendre_values, spectra)
 
 
 def rows_kernel(longitudes_ref, waves_ref, arrived_ref, out_ref, turned, cos_sum, sin_sum):
@@ -105,8 +248,9 @@
             jnp.float32(0.0),
             jnp.where(wave_row == 0, jnp.float32(1.0), jnp.float32(2.0)),
         )
+        values = arrived_ref[slot, 0].reshape(DEVICES, CHANNELS)
         for half in range(2):
-            turned[half] = arrived_ref[slot, 0, pl.ds(half * 128, 128), :].T
+            turned[half] = values[half * 128 : half * 128 + 128, :].T
         real, imag = (
             jnp.concatenate(
                 [turned[half, pl.ds(part, FIELDS, stride=2), :] for half in range(2)], axis=1
@@ -158,7 +302,9 @@
         in_specs=[
             pl.BlockSpec(memory_space=pltpu.SMEM),
             pl.BlockSpec(memory_space=pltpu.VMEM),
-            pl.BlockSpec((SLOTS, 1, DEVICES, CHANNELS), lambda r: (0, r, 0, 0)),
+            pl.BlockSpec(
+                (SLOTS, 1, PLANES, PER_PLANE, LEVS, CHANNELS), lambda r: (0, r, 0, 0, 0, 0)
+            ),
         ],
         out_specs=pl.BlockSpec((1, FIELDS, NLON), lambda r: (r, 0, 0)),
         scratch_shapes=[
@@ -166,7 +312,7 @@
             pltpu.VMEM((STACKED, HALF), jnp.float32),
             pltpu.VMEM((STACKED, HALF), jnp.float32),
         ],
-        compiler_params=pltpu.CompilerParams(vmem_limit_bytes=40 << 20),
+        compiler_params=pltpu.CompilerParams(vmem_limit_bytes=60 << 20),
         interpret=interpret,
     )(row_longitudes, waves, arrived)
 

time: 91.5 us -> 69.7 us (0.76)
  Pallas kernels: 13.9 us -> 68 us
  waiting for transfers between devices: 52.8 us -> 0 us
  starting transfers between devices: 15.7 us -> 0 us
  matrix products: 5.36 us -> 0 us
  local copies, waits for them, and re-layouts: 3.47 us -> 1.57 us
    pallas_call x0 -> x1, Pallas kernels: none -> 53.5 us  [exchange(): pl.pallas_call(exchange_kernel, out_shape=jax.ShapeDtypeStruct(final, jnp...]
    all_to_all x1 -> x0, waiting for transfers between devices: 52.8 us -> none  [exchange(): lax.all_to_all(fourier, ('wave', 'lev'), split_axis=1, concat_axis=1, til...]
    all_to_all x1 -> x0, starting transfers between devices: 15.7 us -> none  [exchange(): lax.all_to_all(fourier, ('wave', 'lev'), split_axis=1, concat_axis=1, til...]
    dot_general x1 -> x0, matrix products: 5.36 us -> none  [legendre_sums(): jnp.einsum('srn,snc->src', legendre_values, kept, preferred_element_type=...]
    dot_general x1 -> x0, local copies, waits for them, and re-layouts: 1.77 us -> none  [legendre_sums(): jnp.einsum('srn,snc->src', legendre_values, kept, preferred_element_type=...]
    reshape x2, local copies, waits for them, and re-layouts: 0.27 us -> 1.57 us  [per_device(): waves = wave_table.reshape(DEVICES, SLOTS).T]
  transfers between devices with their start and end apart: 1 -> 0, of which waited for: 1 -> 0; matrix products, arithmetic and copies ran while one was open for 0% -> 0% of each run, Pallas kernels for 0% -> 0%
where the time goes in v2:
time: 69.7 us; the launch traced here: 69.6 us
  Pallas kernels  68 us (98%)
  local copies, waits for them, and re-layouts  1.57 us (2%)
    pallas_call x1, Pallas kernels, exchange(): pl.pallas_call(exchange_kernel, out_shape=jax.ShapeDtypeStruct(final, jnp...  53.5 us
    pallas_call x1, Pallas kernels, rows_transform(): pl.pallas_call(rows_kernel, out_shape=jax.ShapeDtypeStruct((LOCAL_ROWS, F...  14.4 us
    reshape x2, local copies, waits for them, and re-layouts, per_device(): waves = wave_table.reshape(DEVICES, SLOTS).T  1.57 us

profile of v2, /device:TPU:1, one launch (start us, length us, event | category | flops | bytes accessed | tf_op | source)
XLA Modules:
  0.0 69.6 jit_solution(8247779875363062742)
XLA Ops:
  0.0 0.9 %reshape.3 = s32[256,5]{1,0:T(8,128)S(1)} reshape(s32[1280]{0:T(1024)} %table_ref.1) | data formatting | bytes 10240 | tf_op jit(solution)/shard_map/reshape | solution.py:321
  0.9 0.7 copy.5
  1.6 53.5 %shard_map.46.arrived_ref = f32[5,2,8,4,8,128]{5,4,3,2,1,0:T(8,128)} custom-call(s32[1280]{0:T(1024)} %table_ref.1, bf16[5,512,1280]{2,1,0:T(8,128)(2,1)} %legendre_ref.1, bf16[5,1280,128]{2,1,0:T(8,128)(2,1)} %spectra_ref.1), custom_call_target="tpu_custom_call" | custom-call | tf_op jit(solution)/shard_map/pallas_call | solution.py:198
  55.1 14.4 %shard_map.47 = f32[2,64,5376]{2,1,0:T(8,128)} custom-call(s32[2]{0:T(128)} %longitudes_ref.1, s32[5,256]{1,0:T(8,128)} %bitcast.1, f32[5,2,8,4,8,128]{5,4,3,2,1,0:T(8,128)} %shard_map.46.arrived_ref), custom_call_target="tpu_custom_call" | custom-call | tf_op jit(solution)/shard_map/pallas_call | solution.py:298

commit v3 on v1

v3 whole, which is shorter than its diff:
```python
import jax
import jax.numpy as jnp
from jax import lax
from jax.experimental import pallas as pl
from jax.experimental.pallas import tpu as pltpu
from jax.sharding import PartitionSpec as P

MESH = pl.DeviceIdType.MESH

SLOTS = 5
SLOT_ORDER = (2, 0, 3, 1, 4)
DEGREES = 1280
ROWS = 512
CHANNELS = 128
FIELDS = 64
LOCAL_ROWS = 2
PLANES = 8
PER_PLANE = 4
WAVES = PLANES * PER_PLANE
LEVS = 8
DEVICES = WAVES * LEVS
NLON = 5376
HALF = 256
SPAN = 2 * HALF
BLOCKS = 11
STACKED = BLOCKS * FIELDS

COS_TERMS = (
    0.9999999996168156,
    -19.73920863354667,
    64.93938183835107,
    -85.4564814603686,
    60.24009011425828,
    -26.392650988301078,
    7.765225095262238,
    -1.4134373617596543,
)
SIN_TERMS = (
    6.283185293777215,
    -41.341697721207424,
    81.605000209223,
    -76.70070302960839,
    42.00769493017941,
    -14.834123486306066,
    3.1498534224128543,
)


def horner(terms, square):
    total = jnp.full_like(square, terms[-1])
    for term in terms[-2::-1]:
        total = total * square + jnp.float32(term)
    return total


def cos_sin_of_turns(product, period, inverse):
    whole = jnp.round(product * inverse)
    turn = (product - whole * period) * inverse
    square = turn * turn
    return horner(COS_TERMS, square), turn * horner(SIN_TERMS, square)


def split(values):
    high = values.astype(jnp.bfloat16)
    low = (values - high.astype(jnp.float32)).astype(jnp.bfloat16)
    return high, low


def transform_kernel(
    slot_waves_ref, longitudes_ref, waves_ref, legendre_ref, spectra_ref, out_ref,
    legendre, spectra, fourier, lev_first, x_second, z_first, x_after, final,
    columns, cos_tables, sin_tables, cos_turns, sin_turns, turned, cos_sum, sin_sum, grid,
    load_sem, send_sem, recv_sem, own_sem, out_sem,
):
    wave = lax.axis_index("wave")
    lev = lax.axis_index("lev")
    z, x = lax.div(wave, PER_PLANE), lax.rem(wave, PER_PLANE)
    me = wave * LEVS + lev
    lev_peers = [lax.rem(lev + k, LEVS) for k in range(1, LEVS)]
    x_peers = [lax.rem(x + k, PER_PLANE) for k in range(1, PER_PLANE)]
    z_peers = [lax.rem(z + k, PLANES) for k in (4, 3, 5, 2, 6, 1, 7)]

    def at_lev(peer):
        return wave, peer

    def at_x(peer):
        return z * PER_PLANE + peer, lev

    def at_z(peer):
        return peer * PER_PLANE + x, lev

    def load(slot):
        return (
            pltpu.make_async_copy(spectra_ref.at[slot], spectra.at[slot], load_sem.at[0, slot]),
            pltpu.make_async_copy(legendre_ref.at[slot], legendre.at[slot], load_sem.at[1, slot]),
        )

    for slot in SLOT_ORDER:
        for copy in load(slot):
            copy.start()

    barrier = pltpu.get_barrier_semaphore()
    for peers, at in ((z_peers, at_z), (x_peers, at_x), (lev_peers, at_lev)):
        for peer in peers:
            pl.semaphore_signal(barrier, inc=1, device_id=at(peer), device_id_type=MESH)

    degree = lax.broadcasted_iota(jnp.int32, (DEGREES, CHANNELS), 0)

    def legendre_step(slot):
        for copy in load(slot):
            copy.wait()
        wavenumber = slot_waves_ref[me * SLOTS + slot]
        values = spectra[slot].astype(jnp.float32)
        kept = jnp.where(degree >= wavenumber, values, jnp.float32(0.0)).astype(jnp.bfloat16)
        sums = jnp.dot(legendre[slot], kept, preferred_element_type=jnp.float32)
        fourier[slot] = sums.reshape(WAVES, LEVS * LOCAL_ROWS, CHANNELS)

    def move(stage, slot, source, target, peers, own, at):
        for peer in peers:
            pltpu.make_async_remote_copy(
                src_ref=source(peer),
                dst_ref=target,
                send_sem=send_sem.at[stage],
                recv_sem=recv_sem.at[stage, slot],
                device_id=at(peer),
                device_id_type=MESH,
            ).start()
        pltpu.make_async_copy(source(own), target, own_sem.at[stage, slot]).start()

    def arrived(stage, slot):
        count = 24 if stage == 1 else 28
        region = final.at[slot, pl.ds(0, count)]
        pltpu.make_async_copy(region, region, recv_sem.at[stage, slot]).wait()
        region = final.at[slot, pl.ds(0, WAVES - count)]
        pltpu.make_async_copy(region, region, own_sem.at[stage, slot]).wait()

    def pair(peer):
        return pl.ds(peer * LOCAL_ROWS, LOCAL_ROWS)

    def plane(peer):
        return pl.ds(peer * PER_PLANE, PER_PLANE)

    def first_move(slot):
        if slot < 2:
            move(
                0, slot, lambda peer: fourier.at[slot, plane(peer)],
                z_first.at[slot, z], z_peers, z, at_z,
            )
        else:
            move(
                0, slot, lambda peer: fourier.at[slot, :, pair(peer), :],
                lev_first.at[slot - 2, :, :, lev, :], lev_peers, lev, at_lev,
            )

    def second_move(slot):
        arrived(0, slot)
        if slot < 2:
            move(
                1, slot, lambda peer: z_first.at[slot, :, peer],
                x_after.at[slot, :, x], x_peers, x, at_x,
            )
        else:
            move(
                1, slot,
                lambda peer: lev_first.at[slot - 2].reshape(
                    PLANES, PER_PLANE, LOCAL_ROWS, LEVS, CHANNELS
                ).at[:, peer],
                x_second.at[slot - 2, :, x], x_peers, x, at_x,
            )

    def last_move(slot):
        arrived(1, slot)
        if slot < 2:
            move(
                2, slot,
                lambda peer: x_after.at[slot].reshape(
                    WAVES, LEVS * LOCAL_ROWS, CHANNELS
                ).at[:, pair(peer), :],
                final.at[slot, :, :, lev, :], lev_peers, lev, at_lev,
            )
        else:
            move(
                2, slot, lambda peer: x_second.at[slot - 2, peer],
                final.at[slot, plane(z)], z_peers, z, at_z,
            )

    odd = (2 * lax.broadcasted_iota(jnp.int32, (HALF, HALF), 1) + 1).astype(jnp.float32)
    centre = (
        2 * SPAN * lax.broadcasted_iota(jnp.int32, (16, HALF), 0) + (SPAN - 1)
    ).astype(jnp.float32)

    def spread_waves():
        for part in range(SLOTS * DEVICES // 128):
            row = waves_ref[pl.ds(part, 1), :].astype(jnp.float32)
            columns[pl.ds(part * 128, 128), :] = jnp.broadcast_to(row, (128, 128)).T

    def table_step(row, slot):
        longitudes = longitudes_ref[row]
        period = (2 * longitudes).astype(jnp.float32)
        inverse = (jnp.float32(1.0) / jnp.full((8, 128), period, jnp.float32))[:1, :1]
        largest = lax.div(longitudes - 1, 2).astype(jnp.float32)
        wave_column = columns[pl.ds(slot, DEVICES, stride=SLOTS), :]
        wave_row = jnp.concatenate([wave_column[:128, :].T, wave_column[128:, :].T], axis=1)[:16, :]
        product = jnp.concatenate([wave_column, wave_column], axis=1) * odd
        table_cos, table_sin = cos_sin_of_turns(product, period, inverse)
        for table, tables in ((table_cos, cos_tables), (table_sin, sin_tables)):
            high, low = split(table)
            tables[slot, row, pl.ds(0, HALF), :] = high
            tables[slot, row, pl.ds(HALF, HALF), :] = high
            tables[slot, row, pl.ds(2 * HALF, HALF), :] = low
        weight = jnp.where(
            wave_row > largest,
            jnp.float32(0.0),
            jnp.where(wave_row == 0, jnp.float32(1.0), jnp.float32(2.0)),
        )
        block_cos, block_sin = cos_sin_of_turns(wave_row * centre, period, inverse)
        cos_turns[slot, row] = block_cos * weight
        sin_turns[slot, row] = block_sin * weight

    def add_step(slot, row):
        values = final[slot, :, row].reshape(DEVICES, CHANNELS)
        for half in range(2):
            turned[half] = values[half * 128 : half * 128 + 128, :].T
        real, imag = (
            jnp.concatenate(
                [turned[half, pl.ds(part, FIELDS, stride=2), :] for half in range(2)], axis=1
            )
            for part in range(2)
        )
        block_cos = cos_turns[slot, row]
        block_sin = sin_turns[slot, row]
        real_parts = []
        imag_parts = []
        for k in range(BLOCKS):
            c = block_cos[k : k + 1, :]
            s = block_sin[k : k + 1, :]
            high, low = split(real * c - imag * s)
            real_parts.append(jnp.concatenate([high, low, high], axis=1))
            high, low = split(real * s + imag * c)
            imag_parts.append(jnp.concatenate([high, low, high], axis=1))
        real_side = jnp.concatenate(real_parts, axis=0)
        imag_side = jnp.concatenate(imag_parts, axis=0)
        cos_sum[row] += jnp.dot(
            real_side, cos_tables[slot, row], preferred_element_type=jnp.float32
        )
        sin_sum[row] += jnp.dot(
            imag_side, sin_tables[slot, row], preferred_element_type=jnp.float32
        )

    backwards = 127 - lax.broadcasted_iota(jnp.int32, (FIELDS, 128), 1)
    column = lax.broadcasted_iota(jnp.int32, (FIELDS, 128), 1)

    def finish(row):
        longitudes = longitudes_ref[row]
        for k in range(BLOCKS):
            rows = pl.ds(k * FIELDS, FIELDS)
            for part in range(2):
                lanes = pl.ds(part * 128, 128)
                c = cos_sum[row, rows, lanes]
                s = sin_sum[row, rows, lanes]
                first = k * SPAN + 128 * (1 - part)
                values = jnp.take_along_axis(c + s, backwards, axis=1)
                grid[row, :, pl.ds(first, 128)] = jnp.where(
                    column + first < longitudes, values, jnp.float32(0.0)
                )
                first = k * SPAN + HALF + 128 * part
                if first < NLON:
                    grid[row, :, pl.ds(first, 128)] = jnp.where(
                        column + first < longitudes, c - s, jnp.float32(0.0)
                    )

    def loop(count, act):
        def step(i, carry):
            act(i)
            return carry

        lax.fori_loop(0, count, step, 0)

    legendre_step(SLOT_ORDER[0])
    pl.semaphore_wait(barrier, LEVS + PER_PLANE + PLANES - 3)
    first_move(SLOT_ORDER[0])
    for slot in SLOT_ORDER[1:]:
        legendre_step(slot)
        first_move(slot)
    spread_waves()
    for row in range(LOCAL_ROWS):
        cos_sum[row] = jnp.zeros((STACKED, HALF), jnp.float32)
        sin_sum[row] = jnp.zeros((STACKED, HALF), jnp.float32)
    second_move(2)
    second_move(3)
    loop(SLOTS, lambda slot: table_step(0, slot))
    second_move(0)
    second_move(4)
    last_move(2)
    last_move(3)
    last_move(4)
    loop(SLOTS, lambda slot: table_step(1, slot))
    last_move(0)
    second_move(1)
    last_move(1)

    def slot_step(slot):
        arrived(2, slot)
        loop(LOCAL_ROWS, lambda row: add_step(slot, row))

    loop(SLOTS, slot_step)
    for row in range(LOCAL_ROWS):
        finish(row)
        pltpu.make_async_copy(grid.at[row], out_ref.at[row], out_sem).start()
    for stage in range(3):
        region = final.at[:, pl.ds(0, 24 if stage == 1 else 28)]
        pltpu.make_async_copy(region, region, send_sem.at[stage]).wait()
    pltpu.make_async_copy(grid, out_ref, out_sem).wait()


def transform(wave_table, row_longitudes, legendre_values, spectra):
    hbm = pl.BlockSpec(memory_space=pltpu.HBM)
    smem = pl.BlockSpec(memory_space=pltpu.SMEM)
    tables = pltpu.VMEM((SLOTS, LOCAL_ROWS, 3 * HALF, HALF), jnp.bfloat16)
    turns = pltpu.VMEM((SLOTS, LOCAL_ROWS, 16, HALF), jnp.float32)
    sums = pltpu.VMEM((LOCAL_ROWS, STACKED, HALF), jnp.float32)
    z_then_x = pltpu.VMEM((2, PLANES, PER_PLANE, LEVS * LOCAL_ROWS, CHANNELS), jnp.float32)
    return pl.pallas_call(
        transform_kernel,
        out_shape=jax.ShapeDtypeStruct((LOCAL_ROWS, FIELDS, NLON), jnp.float32),
        in_specs=[smem, smem, pl.BlockSpec(memory_space=pltpu.VMEM), hbm, hbm],
        out_specs=pl.BlockSpec(memory_space=pl.ANY),
        scratch_shapes=[
            pltpu.VMEM((SLOTS, ROWS, DEGREES), jnp.bfloat16),
            pltpu.VMEM((SLOTS, DEGREES, CHANNELS), jnp.bfloat16),
            pltpu.VMEM((SLOTS, WAVES, LEVS * LOCAL_ROWS, CHANNELS), jnp.float32),
            pltpu.VMEM((3, WAVES, LOCAL_ROWS, LEVS, CHANNELS), jnp.float32),
            pltpu.VMEM((3, PLANES, PER_PLANE, LOCAL_ROWS, LEVS, CHANNELS), jnp.float32),
            z_then_x,
            z_then_x,
            pltpu.VMEM((SLOTS, WAVES, LOCAL_ROWS, LEVS, CHANNELS), jnp.float32),
            pltpu.VMEM((SLOTS * DEVICES, 128), jnp.float32),
            tables,
            tables,
            turns,
            turns,
            pltpu.VMEM((2, CHANNELS, 128), jnp.float32),
            sums,
            sums,
            pltpu.VMEM((LOCAL_ROWS, FIELDS, NLON), jnp.float32),
            pltpu.SemaphoreType.DMA((2, SLOTS)),
            pltpu.SemaphoreType.DMA((3,)),
            pltpu.SemaphoreType.DMA((3, SLOTS)),
            pltpu.SemaphoreType.DMA((3, SLOTS)),
            pltpu.SemaphoreType.DMA,
        ],
        compiler_params=pltpu.CompilerParams(
            collective_id=0, has_side_effects=True, vmem_limit_bytes=48 << 20
        ),
    )(
        wave_table,
        row_longitudes,
        wave_table.reshape(SLOTS * DEVICES // 128, 128),
        legendre_values,
        spectra,
    )


def per_device(legendre_values, spectra, wave_table, row_longitudes):
    return transform(wave_table, row_longitudes, legendre_values, spectra)


def solution(mesh):
    in_specs = (
        P(("wave", "lev"), None, None),
        P(("wave", "lev"), None, None),
        P(),
        P(("wave", "lev")),
    )
    out_specs = P(("wave", "lev"), None, None)
    return jax.shard_map(
        per_device, mesh=mesh, in_specs=in_specs, out_specs=out_specs, check_vma=False
    )
```

time: 91.5 us -> 57 us (0.62)
  waiting for transfers between devices: 52.8 us -> 0 us
  Pallas kernels: 13.9 us -> 52.5 us
  starting transfers between devices: 15.7 us -> 0 us
  matrix products: 5.36 us -> 0 us
    all_to_all x1 -> x0, waiting for transfers between devices: 52.8 us -> none  [exchange(): lax.all_to_all(fourier, ('wave', 'lev'), split_axis=1, concat_axis=1, til...]
    pallas_call x1, Pallas kernels: 13.9 us -> 52.5 us  [transform(): pl.pallas_call(transform_kernel, out_shape=jax.ShapeDtypeStruct((LOCAL_RO...]
    all_to_all x1 -> x0, starting transfers between devices: 15.7 us -> none  [exchange(): lax.all_to_all(fourier, ('wave', 'lev'), split_axis=1, concat_axis=1, til...]
    dot_general x1 -> x0, matrix products: 5.36 us -> none  [legendre_sums(): jnp.einsum('srn,snc->src', legendre_values, kept, preferred_element_type=...]
    unnamed x4 -> x7, local copies, waits for them, and re-layouts: 0.23 us -> 4.32 us
    dot_general x1 -> x0, local copies, waits for them, and re-layouts: 1.77 us -> none  [legendre_sums(): jnp.einsum('srn,snc->src', legendre_values, kept, preferred_element_type=...]
  transfers between devices with their start and end apart: 1 -> 0, of which waited for: 1 -> 0; matrix products, arithmetic and copies ran while one was open for 0% -> 0% of each run, Pallas kernels for 0% -> 0%
where the time goes in v3:
time: 57 us; the launch traced here: 56.9 us
  Pallas kernels  52.5 us (92%)
  local copies, waits for them, and re-layouts  4.32 us (8%)
    pallas_call x1, Pallas kernels, transform(): pl.pallas_call(transform_kernel, out_shape=jax.ShapeDtypeStruct((LOCAL_RO...  52.5 us
    unnamed x7, local copies, waits for them, and re-layouts  4.32 us

profile of v3, /device:TPU:1, one launch (start us, length us, event | category | flops | bytes accessed | tf_op | source)
XLA Modules:
  0.0 56.9 jit_solution(14277265099056991962)
XLA Ops:
  0.0 0.0 copy-start
  0.0 1.4 %copy-done = bf16[5,1280,128]{2,1,0:T(8,128)(2,1)S(1)} copy-done((bf16[5,1280,128]{2,1,0:T(8,128)(2,1)S(1)}, bf16[5,1280,128]{2,1,0:T(8,128)(2,1)}, u32[]{:S(2)}) %copy-start) | copy-done | bytes 1638424
  1.4 0.0 copy-start.1
  1.4 0.7 %copy-done.1 = s32[1280]{0:T(1024)S(1)} copy-done((s32[1280]{0:T(1024)S(1)}, s32[1280]{0:T(1024)}, u32[]{:S(2)}) %copy-start.1) | copy-done | bytes 5144
  2.1 0.0 copy-start.2
  2.1 0.7 %copy-done.2 = s32[2]{0:T(128)S(1)} copy-done((s32[2]{0:T(128)S(1)}, s32[2]{0:T(128)}, u32[]{:S(2)}) %copy-start.2) | copy-done | bytes 32
  2.8 52.5 %shard_map.46 = f32[2,64,5376]{2,1,0:T(8,128)S(1)} custom-call(s32[1280]{0:T(1024)S(1)} %copy-done.1, s32[2]{0:T(128)S(1)} %copy-done.2, s32[10,128]{1,0:T(8,128)S(1)} %bitcast.1, bf16[5,512,1280]{2,1,0:T(8,128)(2,1)} %legendre_ref.1, bf16[5,1280,128]{2,1,0:T(8,128)(2,1)S(1)} %copy-done), custom_call_target="tpu_custom_call" | custom-call | tf_op jit(solution)/shard_map/pallas_call | solution.py:323
  55.3 1.5 %copy.6 = f32[2,64,5376]{2,1,0:T(8,128)} copy(f32[2,64,5376]{2,1,0:T(8,128)S(1)} %shard_map.46) | data formatting | bytes 5505024
Async XLA Ops:
  0.0 1.4 %copy-start = (bf16[5,1280,128]{2,1,0:T(8,128)(2,1)S(1)}, bf16[5,1280,128]{2,1,0:T(8,128)(2,1)}, u32[]{:S(2)}) copy-start(bf16[5,1280,128]{2,1,0:T(8,128)(2,1)} %spectra_ref.1) | copy-start | bytes 4915204
  1.4 0.7 %copy-start.1 = (s32[1280]{0:T(1024)S(1)}, s32[1280]{0:T(1024)}, u32[]{:S(2)}) copy-start(s32[1280]{0:T(1024)} %slot_waves_ref.1) | copy-start | bytes 15364
  2.1 0.7 %copy-start.2 = (s32[2]{0:T(128)S(1)}, s32[2]{0:T(128)}, u32[]{:S(2)}) copy-start(s32[2]{0:T(128)} %longitudes_ref.1) | copy-start | bytes 28

commit v4 on v3

--- a/solution.py
+++ b/solution.py
@@ -8,7 +8,6 @@
 MESH = pl.DeviceIdType.MESH
 
 SLOTS = 5
-SLOT_ORDER = (2, 0, 3, 1, 4)
 DEGREES = 1280
 ROWS = 512
 CHANNELS = 128
@@ -95,7 +94,7 @@
             pltpu.make_async_copy(legendre_ref.at[slot], legendre.at[slot], load_sem.at[1, slot]),
         )
 
-    for slot in SLOT_ORDER:
+    for slot in range(SLOTS):
         for copy in load(slot):
             copy.start()
 
@@ -141,46 +140,46 @@
         return pl.ds(peer * PER_PLANE, PER_PLANE)
 
     def first_move(slot):
-        if slot < 2:
+        if slot % 2:
             move(
                 0, slot, lambda peer: fourier.at[slot, plane(peer)],
-                z_first.at[slot, z], z_peers, z, at_z,
+                z_first.at[slot // 2, z], z_peers, z, at_z,
             )
         else:
             move(
                 0, slot, lambda peer: fourier.at[slot, :, pair(peer), :],
-                lev_first.at[slot - 2, :, :, lev, :], lev_peers, lev, at_lev,
+                lev_first.at[slot // 2, :, :, lev, :], lev_peers, lev, at_lev,
             )
 
     def second_move(slot):
         arrived(0, slot)
-        if slot < 2:
-            move(
-                1, slot, lambda peer: z_first.at[slot, :, peer],
-                x_after.at[slot, :, x], x_peers, x, at_x,
+        if slot % 2:
+            move(
+                1, slot, lambda peer: z_first.at[slot // 2, :, peer],
+                x_after.at[slot // 2, :, x], x_peers, x, at_x,
             )
         else:
             move(
                 1, slot,
-                lambda peer: lev_first.at[slot - 2].reshape(
+                lambda peer: lev_first.at[slot // 2].reshape(
                     PLANES, PER_PLANE, LOCAL_ROWS, LEVS, CHANNELS
                 ).at[:, peer],
-                x_second.at[slot - 2, :, x], x_peers, x, at_x,
+                x_second.at[slot // 2, :, x], x_peers, x, at_x,
             )
 
     def last_move(slot):
         arrived(1, slot)
-        if slot < 2:
+        if slot % 2:
             move(
                 2, slot,
-                lambda peer: x_after.at[slot].reshape(
+                lambda peer: x_after.at[slot // 2].reshape(
                     WAVES, LEVS * LOCAL_ROWS, CHANNELS
                 ).at[:, pair(peer), :],
                 final.at[slot, :, :, lev, :], lev_peers, lev, at_lev,
             )
         else:
             move(
-                2, slot, lambda peer: x_second.at[slot - 2, peer],
+                2, slot, lambda peer: x_second.at[slot // 2, peer],
                 final.at[slot, plane(z)], z_peers, z, at_z,
             )
 
@@ -276,28 +275,28 @@
 
         lax.fori_loop(0, count, step, 0)
 
-    legendre_step(SLOT_ORDER[0])
+    legendre_step(0)
     pl.semaphore_wait(barrier, LEVS + PER_PLANE + PLANES - 3)
-    first_move(SLOT_ORDER[0])
-    for slot in SLOT_ORDER[1:]:
+    first_move(0)
+    for slot in range(1, SLOTS):
         legendre_step(slot)
         first_move(slot)
     spread_waves()
     for row in range(LOCAL_ROWS):
         cos_sum[row] = jnp.zeros((STACKED, HALF), jnp.float32)
         sin_sum[row] = jnp.zeros((STACKED, HALF), jnp.float32)
+    second_move(0)
     second_move(2)
+    loop(SLOTS, lambda slot: table_step(0, slot))
+    second_move(1)
+    second_move(4)
+    last_move(0)
+    last_move(2)
     second_move(3)
-    loop(SLOTS, lambda slot: table_step(0, slot))
-    second_move(0)
-    second_move(4)
-    last_move(2)
+    last_move(4)
+    last_move(1)
+    loop(SLOTS, lambda slot: table_step(1, slot))
     last_move(3)
-    last_move(4)
-    loop(SLOTS, lambda slot: table_step(1, slot))
-    last_move(0)
-    second_move(1)
-    last_move(1)
 
     def slot_step(slot):
         arrived(2, slot)
@@ -353,11 +352,16 @@
             collective_id=0, has_side_effects=True, vmem_limit_bytes=48 << 20
         ),
     )(
-        wave_table,
-        row_longitudes,
-        wave_table.reshape(SLOTS * DEVICES // 128, 128),
-        legendre_values,
-        spectra,
+        *(
+            pltpu.with_memory_space_constraint(operand, pltpu.HBM)
+            for operand in (
+                wave_table,
+                row_longitudes,
+                wave_table.reshape(SLOTS * DEVICES // 128, 128),
+                legendre_values,
+                spectra,
+            )
+        )
     )
 
 

time: 57 us -> 46.3 us (0.81)
  Pallas kernels: 52.5 us -> 44.6 us
  local copies, waits for them, and re-layouts: 4.32 us -> 1.54 us
    pallas_call x1, Pallas kernels: 52.5 us -> 44.6 us  [transform(): pl.pallas_call(transform_kernel, out_shape=jax.ShapeDtypeStruct((LOCAL_RO...]
    unnamed x7 -> x1, local copies, waits for them, and re-layouts: 4.32 us -> 1.54 us
where the time goes in v4:
time: 46.3 us; the launch traced here: 46.2 us
  Pallas kernels  44.6 us (96%)
  local copies, waits for them, and re-layouts  1.54 us (3%)
    pallas_call x1, Pallas kernels, transform(): pl.pallas_call(transform_kernel, out_shape=jax.ShapeDtypeStruct((LOCAL_RO...  44.6 us
    unnamed x1, local copies, waits for them, and re-layouts  1.54 us

profile of v4, /device:TPU:1, one launch (start us, length us, event | category | flops | bytes accessed | tf_op | source)
XLA Modules:
  0.0 46.2 jit_solution(599800349200197562)
XLA Ops:
  0.0 44.6 %shard_map.46 = f32[2,64,5376]{2,1,0:T(8,128)S(1)} custom-call(s32[1280]{0:T(1024)} %slot_waves_ref.1, s32[2]{0:T(128)} %longitudes_ref.1, s32[10,128]{1,0:T(8,128)} %bitcast.1, bf16[5,512,1280]{2,1,0:T(8,128)(2,1)} %legendre_ref.1, bf16[5,1280,128]{2,1,0:T(8,128)(2,1)} %spectra_ref.1), custom_call_target="tpu_custom_call" | custom-call | tf_op jit(solution)/shard_map/pallas_call | solution.py:322
  44.6 1.5 %copy.6 = f32[2,64,5376]{2,1,0:T(8,128)} copy(f32[2,64,5376]{2,1,0:T(8,128)S(1)} %shard_map.46) | data formatting | bytes 5505024

commit v5 on v4

--- a/solution.py
+++ b/solution.py
@@ -68,8 +68,8 @@
 def transform_kernel(
     slot_waves_ref, longitudes_ref, waves_ref, legendre_ref, spectra_ref, out_ref,
     legendre, spectra, fourier, lev_first, x_second, z_first, x_after, final,
-    columns, cos_tables, sin_tables, cos_turns, sin_turns, turned, cos_sum, sin_sum, grid,
-    load_sem, send_sem, recv_sem, own_sem, out_sem,
+    columns, cos_tables, sin_tables, cos_turns, sin_turns, turned, cos_sum, sin_sum,
+    load_sem, send_sem, recv_sem, own_sem,
 ):
     wave = lax.axis_index("wave")
     lev = lax.axis_index("lev")
@@ -259,12 +259,12 @@
                 s = sin_sum[row, rows, lanes]
                 first = k * SPAN + 128 * (1 - part)
                 values = jnp.take_along_axis(c + s, backwards, axis=1)
-                grid[row, :, pl.ds(first, 128)] = jnp.where(
+                out_ref[row, :, pl.ds(first, 128)] = jnp.where(
                     column + first < longitudes, values, jnp.float32(0.0)
                 )
                 first = k * SPAN + HALF + 128 * part
                 if first < NLON:
-                    grid[row, :, pl.ds(first, 128)] = jnp.where(
+                    out_ref[row, :, pl.ds(first, 128)] = jnp.where(
                         column + first < longitudes, c - s, jnp.float32(0.0)
                     )
 
@@ -302,14 +302,16 @@
         arrived(2, slot)
         loop(LOCAL_ROWS, lambda row: add_step(slot, row))
 
-    loop(SLOTS, slot_step)
-    for row in range(LOCAL_ROWS):
+    def last_step(row):
+        add_step(SLOTS - 1, row)
         finish(row)
-        pltpu.make_async_copy(grid.at[row], out_ref.at[row], out_sem).start()
+
+    loop(SLOTS - 1, slot_step)
+    arrived(2, SLOTS - 1)
+    loop(LOCAL_ROWS, last_step)
     for stage in range(3):
         region = final.at[:, pl.ds(0, 24 if stage == 1 else 28)]
         pltpu.make_async_copy(region, region, send_sem.at[stage]).wait()
-    pltpu.make_async_copy(grid, out_ref, out_sem).wait()
 
 
 def transform(wave_table, row_longitudes, legendre_values, spectra):
@@ -323,7 +325,7 @@
         transform_kernel,
         out_shape=jax.ShapeDtypeStruct((LOCAL_ROWS, FIELDS, NLON), jnp.float32),
         in_specs=[smem, smem, pl.BlockSpec(memory_space=pltpu.VMEM), hbm, hbm],
-        out_specs=pl.BlockSpec(memory_space=pl.ANY),
+        out_specs=pl.BlockSpec(memory_space=pltpu.VMEM),
         scratch_shapes=[
             pltpu.VMEM((SLOTS, ROWS, DEGREES), jnp.bfloat16),
             pltpu.VMEM((SLOTS, DEGREES, CHANNELS), jnp.bfloat16),
@@ -341,12 +343,10 @@
             pltpu.VMEM((2, CHANNELS, 128), jnp.float32),
             sums,
             sums,
-            pltpu.VMEM((LOCAL_ROWS, FIELDS, NLON), jnp.float32),
             pltpu.SemaphoreType.DMA((2, SLOTS)),
             pltpu.SemaphoreType.DMA((3,)),
             pltpu.SemaphoreType.DMA((3, SLOTS)),
             pltpu.SemaphoreType.DMA((3, SLOTS)),
-            pltpu.SemaphoreType.DMA,
         ],
         compiler_params=pltpu.CompilerParams(
             collective_id=0, has_side_effects=True, vmem_limit_bytes=48 << 20

time: 46.3 us -> 45.5 us (0.983)
  Pallas kernels: 44.6 us -> 43.8 us
    pallas_call x1, Pallas kernels: 44.6 us -> 43.8 us  [transform(): pl.pallas_call(transform_kernel, out_shape=jax.ShapeDtypeStruct((LOCAL_RO...]
where the time goes in v5:
time: 45.5 us; the launch traced here: 45.4 us
  Pallas kernels  43.8 us (96%)
  local copies, waits for them, and re-layouts  1.54 us (3%)
    pallas_call x1, Pallas kernels, transform(): pl.pallas_call(transform_kernel, out_shape=jax.ShapeDtypeStruct((LOCAL_RO...  43.8 us
    unnamed x1, local copies, waits for them, and re-layouts  1.54 us

profile of v5, /device:TPU:1, one launch (start us, length us, event | category | flops | bytes accessed | tf_op | source)
XLA Modules:
  0.0 45.4 jit_solution(10320098582040393916)
XLA Ops:
  0.0 43.8 %shard_map.46 = f32[2,64,5376]{2,1,0:T(8,128)S(1)} custom-call(s32[1280]{0:T(1024)} %slot_waves_ref.1, s32[2]{0:T(128)} %longitudes_ref.1, s32[10,128]{1,0:T(8,128)} %bitcast.1, bf16[5,512,1280]{2,1,0:T(8,128)(2,1)} %legendre_ref.1, bf16[5,1280,128]{2,1,0:T(8,128)(2,1)} %spectra_ref.1), custom_call_target="tpu_custom_call" | custom-call | tf_op jit(solution)/shard_map/pallas_call | solution.py:324
  43.8 1.5 %copy.6 = f32[2,64,5376]{2,1,0:T(8,128)} copy(f32[2,64,5376]{2,1,0:T(8,128)S(1)} %shard_map.46) | data formatting | bytes 5505024

commit v6 on v5

--- a/solution.py
+++ b/solution.py
@@ -308,7 +308,8 @@
 
     loop(SLOTS - 1, slot_step)
     arrived(2, SLOTS - 1)
-    loop(LOCAL_ROWS, last_step)
+    for row in range(LOCAL_ROWS):
+        last_step(row)
     for stage in range(3):
         region = final.at[:, pl.ds(0, 24 if stage == 1 else 28)]
         pltpu.make_async_copy(region, region, send_sem.at[stage]).wait()

time: 45.5 us -> 45.4 us (level)
  no operation moved by 1% of the time
where the time goes in v6:
time: 45.4 us; the launch traced here: 45.2 us
  Pallas kernels  43.7 us (96%)
  local copies, waits for them, and re-layouts  1.54 us (3%)
    pallas_call x1, Pallas kernels, transform(): pl.pallas_call(transform_kernel, out_shape=jax.ShapeDtypeStruct((LOCAL_RO...  43.7 us
    unnamed x1, local copies, waits for them, and re-layouts  1.54 us

profile of v6, /device:TPU:1, one launch (start us, length us, event | category | flops | bytes accessed | tf_op | source)
XLA Modules:
  0.0 45.2 jit_solution(9690570574528882186)
XLA Ops:
  0.0 43.7 %shard_map.46 = f32[2,64,5376]{2,1,0:T(8,128)S(1)} custom-call(s32[1280]{0:T(1024)} %slot_waves_ref.1, s32[2]{0:T(128)} %longitudes_ref.1, s32[10,128]{1,0:T(8,128)} %bitcast.1, bf16[5,512,1280]{2,1,0:T(8,128)(2,1)} %legendre_ref.1, bf16[5,1280,128]{2,1,0:T(8,128)(2,1)} %spectra_ref.1), custom_call_target="tpu_custom_call" | custom-call | tf_op jit(solution)/shard_map/pallas_call | solution.py:325
  43.7 1.5 %copy.6 = f32[2,64,5376]{2,1,0:T(8,128)} copy(f32[2,64,5376]{2,1,0:T(8,128)S(1)} %shard_map.46) | data formatting | bytes 5505024
